TPU v7x, 32 devices: a whole 2x2x4 slice. The times are simulated.
32 devices in a mesh: lon: 8 (over y, x, core), lat: 4 (over z).
Axes of the slice: x: 2, y: 2, z: 4, core: 2. Of those that a mesh axis runs over, the one named last changes fastest.
Arguments:
- checkpoint: float32 [4, 256, 9600], P('lat', 'lon'), may hold values from -6 to 6
- slot_dest: int32 [4, 256], P('lat'), may hold values from -1 to 255, as said below
- kmt: int32 [640, 3840], P('lat', 'lon'), may hold values from 0 to 2, as said below
- kappa: float32 [2, 640, 3840], P(None, 'lat', 'lon'), may hold values from 0.02 to 0.2
Outputs:
- new_tracer: float32 [2, 2, 640, 3840], P(None, None, 'lat', 'lon')
- stream: float32 [640, 3840], P('lat', 'lon')
Inputs may be any that keep to these rules, and one draw needn't show every extreme that they name: `slot_dest`: in each band every value e * 32 + p is named by at most one slot; at most 4 slots of one checkpoint owner's 32 slots name one new owner e, and exactly 4 for some pair in every band. Positions that no slot names are land blocks. kmt is 0 on every point of a land block.
All inputs are finite; a program needn't handle non-finite values.
Results may differ from a plain program's by a relative error of at most 0.0001.
Values sent between devices are 32-bit elements; how exact they have to be, the bound alone decides.
No kernel may reach another device: no remote copies, remote signals or barrier semaphores. Data moves between devices by JAX's collectives and lax.ppermute only.
A program may use at most 128 MiB of HBM per device.

v0:
```python
import jax
import jax.numpy as jnp
from jax import lax
from jax.sharding import PartitionSpec as P

BH = 40
BW = 60
LEV = 2
ITERS = 3
thermal = 0.25
haline = 0.75
cabbeling = 0.05


def extended(value, sides, width, wrap):
    for axis, dim in sides:
        size, length = (lax.axis_size(axis), value.shape[dim])
        up = [(i, (i + 1) % size) for i in range(size if wrap else size - 1)]
        down = [(j, i) for i, j in up]
        last = lax.slice_in_dim(value, length - width, length, axis=dim)
        initial = lax.slice_in_dim(value, 0, width, axis=dim)
        before = lax.ppermute(last, axis, up)
        after = lax.ppermute(initial, axis, down)
        value = jnp.concatenate([before, value, after], axis=dim)
    return value


def extend(field):
    beside_all = extended(field, (("lon", 2),), 1, True)
    return extended(beside_all, (("lat", 1),), 1, False)


def operate(vector, depth, column):
    wide = extend(vector[None])[0]
    edges = wide[2:, 1:-1] + wide[:-2, 1:-1] + wide[1:-1, 2:] + wide[1:-1, :-2]
    corners = wide[2:, 2:] + wide[2:, :-2] + wide[:-2, 2:] + wide[:-2, :-2]
    return column * ((6.0 + depth) * vector - edges - 0.5 * corners)


def squares(residual):
    return lax.psum(jnp.sum(residual * residual), ("lon", "lat"))


def body(checkpoint, slot_dest, kmt, kappa):
    myself = lax.axis_index("lon")
    blocks = checkpoint[0]
    dest_all = slot_dest[0]
    slots_dev = blocks.shape[0]
    values_blk = blocks.shape[1]
    owner = jnp.where(dest_all >= 0, dest_all // slots_dev, -1)
    landing = jnp.where(dest_all >= 0, dest_all % slots_dev, 0)
    empty = jnp.zeros((slots_dev + 1, values_blk), jnp.float32)
    target = jnp.where(owner == myself, landing, slots_dev)
    placed = empty.at[target].set(lax.all_gather(blocks, "lon", axis=0, tiled=True))[:slots_dev]
    rows_dev = kmt.shape[0]
    cols_dev = kmt.shape[1]
    block_rows = rows_dev // BH
    block_cols = cols_dev // BW
    field = placed.reshape(block_rows, block_cols, 2, LEV, BH, BW)
    field = field.transpose(2, 3, 0, 4, 1, 5).reshape(2, LEV, rows_dev, cols_dev)
    levels = jnp.arange(LEV, dtype=jnp.int32)
    wet = (levels[:, None, None] < kmt[None]).astype(jnp.float32)
    tracer = field * wet
    stacked = jnp.concatenate([tracer.reshape(2 * LEV, rows_dev, cols_dev), wet, kappa], axis=0)
    wide = extend(stacked)
    tracer_w = wide[: 2 * LEV].reshape(2, LEV, rows_dev + 2, cols_dev + 2)
    wet_w = wide[2 * LEV : 3 * LEV]
    kappa_w = wide[3 * LEV :]
    tracer_c = tracer_w[..., 1:-1, 1:-1]
    wet_c = wet_w[:, 1:-1, 1:-1]
    kappa_c = kappa_w[:, 1:-1, 1:-1]
    change = jnp.zeros_like(tracer)
    for step_y, step_x in ((0, 1), (0, -1), (1, 0), (-1, 0)):
        rows = slice(1 + step_y, 1 + step_y + rows_dev)
        cols = slice(1 + step_x, 1 + step_x + cols_dev)
        face = 0.5 * (kappa_c + kappa_w[:, rows, cols]) * wet_c * wet_w[:, rows, cols]
        change = change + face * (tracer_w[..., rows, cols] - tracer_c)
    new_tracer = wet * (tracer + change)
    thickness = 1.0 + 0.5 * jnp.arange(LEV, dtype=jnp.float32)
    temp = new_tracer[0]
    salt = new_tracer[1]
    density = wet * (haline * salt - thermal * temp - cabbeling * temp * temp)
    forcing = jnp.sum(thickness[:, None, None] * density, axis=0)
    depth = jnp.sum(thickness[:, None, None] * wet, axis=0)
    column = (kmt > 0).astype(jnp.float32)
    stream = jnp.zeros_like(forcing)
    residual = column * forcing
    direction = residual
    norm_now = squares(residual)
    for step in range(ITERS):
        image = operate(direction, depth, column)
        alpha = norm_now / lax.psum(jnp.sum(direction * image), ("lon", "lat"))
        stream = stream + alpha * direction
        residual = residual - alpha * image
        norm_next = squares(residual)
        direction = residual + norm_next / norm_now * direction
        norm_now = norm_next
    return (new_tracer, stream)


def solution(mesh):
    placed = (P("lat", "lon", None), P("lat", None), P("lat", "lon"), P(None, "lat", "lon"))
    return jax.shard_map(
        body,
        mesh=mesh,
        in_specs=placed,
        out_specs=(P(None, None, "lat", "lon"), P("lat", "lon")),
        check_vma=False,
    )
```

profile of v0, /device:TPU:0, one launch (start us, length us, event | category | flops | bytes accessed | tf_op | source)
XLA Modules:
  0.0 378.9 jit_solution(3048188095001395048)
XLA Ops:
  7.2 0.7 all-gather.3.cloned.1.call-update
  7.9 0.7 compare_select_fusion
  8.7 64.3 %all-gather.3.cloned.1.call-done = f32[1,256,9600]{2,1,0:T(8,128)} async-done(((f32[1,32,9600]{2,1,0:T(8,128)}), f32[1,256,9600]{2,1,0:T(8,128)}) %all-gather.3.cloned.1.call-update) | async-done | bytes 9830416 | tf_op jit(solution)/shard_map/all_gather | solution.py:54
  73.0 10.2 %scatter_custom_fusion = f32[33,9600]{1,0:T(8,128)S(1)} fusion(s32[256]{0:T(256)S(1)} %bitcast.51, f32[1,256,9600]{2,1,0:T(8,128)} %all-gather.3.cloned.1.call-done, f32[]{:T(128)} %constant.51.clone.1), kind=kCustom, calls=%fused_computation.1 | custom fusion | bytes 11097604 | tf_op jit(solution)/shard_map/scatter | solution.py:54
  83.3 5.4 %reshape.159 = f32[4,8,2,2,40,60]{5,4,3,2,1,0:T(8,128)} reshape(f32[32,9600]{1,0:T(8,128)S(1)} %slice.258) | data formatting | bytes 2457600 | tf_op jit(solution)/shard_map/reshape | solution.py:59
  88.7 3.3 copy.8
  92.0 1.5 copy-done
  93.5 1.7 reshape.161
  95.3 1.6 bitcast_multiply_fusion
  97.8 1.3 collective-permute-start
  99.1 2.9 reshape.160
  102.1 1.0 collective-permute-done.1
  103.7 1.0 pad_maximum_fusion.29
  104.7 1.3 collective-permute-start.3
  106.0 0.8 fusion.27
  106.9 4.5 %collective-permute-start.2 = (f32[8,1,482]{2,1,0:T(1,128)S(1)}, f32[8,1,482]{2,1,0:T(1,128)S(1)}, u32[]{:S(2)}, u32[]{:S(2)}) collective-permute-start(f32[8,1,482]{2,1,0:T(1,128)S(1)} %get-tuple-element.15), channel_id=1, source_target_pairs={{0,1},{1,2},{2,3},{4,5},{5,6},{6,7},{8,9},{9,10},{10,11},{12,13},{... | collective-permute-start | bytes 46280 | tf_op jit(solution)/shard_map/ppermute | solution.py:22
  111.4 0.4 fusion.21
  111.8 1.0 collective-permute-done.2
  113.2 0.5 pad_maximum_fusion
  113.8 0.8 copy-done.6
  114.5 1.4 fusion.5
  116.4 0.7 copy-done.5
  117.2 2.6 collective-permute-start.5
  119.8 2.5 collective-permute-done.4
  122.5 4.2 %collective-permute-start.6 = (f32[1,1,482]{2,1,0:T(1,128)S(1)}, f32[1,1,482]{2,1,0:T(1,128)S(1)}, u32[]{:S(2)}, u32[]{:S(2)}) collective-permute-start(f32[1,1,482]{2,1,0:T(1,128)S(1)} %get-tuple-element.25), channel_id=1, source_target_pairs={{0,1},{1,2},{2,3},{4,5},{5,6},{6,7},{8,9},{9,10},{10,11},{12,13},{... | collective-permute-start | bytes 5792 | tf_op jit(solution)/shard_map/ppermute | solution.py:22
  126.7 1.5 collective-permute-start.7
  128.2 3.9 %collective-permute-done.7 = f32[1,1,482]{2,1,0:T(1,128)S(1)} collective-permute-done((f32[1,1,482]{2,1,0:T(1,128)S(1)}, f32[1,1,482]{2,1,0:T(1,128)S(1)}, u32[]{:S(2)}, u32[]{:S(2)}) %collective-permute-start.7) | collective-permute-done | bytes 1960 | tf_op jit(solution)/shard_map/ppermute | solution.py:23
  132.3 1.1 multiply_reduce_fusion.3
  133.4 39.5 %all-reduce = (f32[]{:T(128)}, f32[]{:T(128)}) all-reduce(f32[]{:T(128)} %get-tuple-element.3, f32[]{:T(128)} %get-tuple-element.2), channel_id=1, replica_groups=mesh['lon'=8,'lat'=4] {'lon','lat'}, use_global_device_ids=true, to_apply=%region_3.4 | all-reduce | flops 2 | bytes 16 | tf_op jit(solution)/shard_map/psum | solution.py:41
  174.3 0.7 multiply_reduce_fusion.2
  175.0 39.9 %psum.44 = f32[]{:T(128)} all-reduce(f32[]{:T(128)} %get-tuple-element.10), channel_id=1, replica_groups=mesh['lon'=8,'lat'=4] {'lon','lat'}, use_global_device_ids=true, to_apply=%region_8.9 | all-reduce | flops 1 | bytes 8 | tf_op jit(solution)/shard_map/psum | solution.py:41
  216.4 2.6 collective-permute-start.9
  219.0 2.1 collective-permute-done.8
  221.2 3.5 collective-permute-start.10
  224.7 1.3 collective-permute-start.11
  226.0 4.2 %collective-permute-done.11 = f32[1,1,482]{2,1,0:T(1,128)S(1)} collective-permute-done((f32[1,1,482]{2,1,0:T(1,128)S(1)}, f32[1,1,482]{2,1,0:T(1,128)S(1)}, u32[]{:S(2)}, u32[]{:S(2)}) %collective-permute-start.11) | collective-permute-done | bytes 1960 | tf_op jit(solution)/shard_map/ppermute | solution.py:23
  230.4 1.1 multiply_reduce_fusion.1
  231.5 40.0 %psum.45 = f32[]{:T(128)} all-reduce(f32[]{:T(128)} %get-tuple-element.8), channel_id=1, replica_groups=mesh['lon'=8,'lat'=4] {'lon','lat'}, use_global_device_ids=true, to_apply=%region_10.11 | all-reduce | flops 1 | bytes 8 | tf_op jit(solution)/shard_map/psum | solution.py:92
  272.8 0.7 multiply_reduce_fusion
  273.5 40.8 %psum.46 = f32[]{:T(128)} all-reduce(f32[]{:T(128)} %multiply_reduce_fusion), channel_id=1, replica_groups=mesh['lon'=8,'lat'=4] {'lon','lat'}, use_global_device_ids=true, to_apply=%region_12.13 | all-reduce | flops 1 | bytes 8 | tf_op jit(solution)/shard_map/psum | solution.py:41
  315.8 2.6 collective-permute-start.13
  318.4 2.1 collective-permute-done.12
  320.6 3.3 collective-permute-start.14
  323.9 1.3 collective-permute-start.15
  325.2 4.2 %collective-permute-done.15 = f32[1,1,482]{2,1,0:T(1,128)S(1)} collective-permute-done((f32[1,1,482]{2,1,0:T(1,128)S(1)}, f32[1,1,482]{2,1,0:T(1,128)S(1)}, u32[]{:S(2)}, u32[]{:S(2)}) %collective-permute-start.15) | collective-permute-done | bytes 1960 | tf_op jit(solution)/shard_map/ppermute | solution.py:23
  329.6 1.1 fusion.35
  330.7 39.3 %psum.47 = f32[]{:T(128)} all-reduce(f32[]{:T(128)} %fusion.35), channel_id=1, replica_groups=mesh['lon'=8,'lat'=4] {'lon','lat'}, use_global_device_ids=true, to_apply=%region_14.15 | all-reduce | flops 1 | bytes 8 | tf_op jit(solution)/shard_map/psum | solution.py:92
  371.2 0.8 multiply_add_fusion
  (46 shorter events, 3.8 us)
Async XLA Ops:
  7.2 1.4 copy-start.3
  7.2 65.8 %all-gather.3.cloned.1.call-start = ((), (), s32[]{:S(2)}) async-start(), calls=%async_computation | async-start | bytes 11059200 | tf_op jit(solution)/shard_map/all_gather | solution.py:54
  92.0 1.5 copy-start
  95.3 1.6 copy-start.1
  97.8 5.6 %collective-permute-start = (f32[8,160,1]{1,0,2:T(8,128)S(1)}, f32[8,160,1]{1,0,2:T(8,128)S(1)}, u32[]{:S(2)}, u32[]{:S(2)}) collective-permute-start(f32[8,160,1]{1,0,2:T(8,128)S(1)} %copy.10), channel_id=1, source_target_pairs={{4,0},{8,4},{12,8},{16,12},{20,16},{24,20},{28,24},{0,28},{5,1},{9... | collective-permute-start | bytes 15368 | tf_op jit(solution)/shard_map/ppermute | solution.py:23
  99.1 4.0 %collective-permute-start.1 = (f32[8,160,1]{1,0,2:T(8,128)S(1)}, f32[8,160,1]{1,0,2:T(8,128)S(1)}, u32[]{:S(2)}, u32[]{:S(2)}) collective-permute-start(f32[8,160,1]{1,0,2:T(8,128)S(1)} %copy.12), channel_id=1, source_target_pairs={{0,4},{4,8},{8,12},{12,16},{16,20},{20,24},{24,28},{28,0},{1,5},{5... | collective-permute-start | bytes 15368 | tf_op jit(solution)/shard_map/ppermute | solution.py:22
  103.7 2.3 copy-start.2
  103.7 2.3 copy-start.4
  104.7 6.7 %collective-permute-start.3 = (f32[8,1,482]{2,1,0:T(1,128)S(1)}, f32[8,1,482]{2,1,0:T(1,128)S(1)}, u32[]{:S(2)}, u32[]{:S(2)}) collective-permute-start(f32[8,1,482]{2,1,0:T(1,128)S(1)} %get-tuple-element.16), channel_id=1, source_target_pairs={{1,0},{2,1},{3,2},{5,4},{6,5},{7,6},{9,8},{10,9},{11,10},{13,12},{... | collective-permute-start | bytes 46280 | tf_op jit(solution)/shard_map/ppermute | solution.py:23
  106.9 6.0 %collective-permute-start.2 = (f32[8,1,482]{2,1,0:T(1,128)S(1)}, f32[8,1,482]{2,1,0:T(1,128)S(1)}, u32[]{:S(2)}, u32[]{:S(2)}) collective-permute-start(f32[8,1,482]{2,1,0:T(1,128)S(1)} %get-tuple-element.15), channel_id=1, source_target_pairs={{0,1},{1,2},{2,3},{4,5},{5,6},{6,7},{8,9},{9,10},{10,11},{12,13},{... | collective-permute-start | bytes 46280 | tf_op jit(solution)/shard_map/ppermute | solution.py:22
  113.2 1.3 copy-start.6
  116.0 1.1 copy-start.5
  117.1 5.2 %collective-permute-start.4 = (f32[1,160,1]{2,1,0:T(8,128)S(1)}, f32[1,160,1]{2,1,0:T(8,128)S(1)}, u32[]{:S(2)}, u32[]{:S(2)}) collective-permute-start(f32[1,160,1]{2,1,0:T(8,128)S(1)} %get-tuple-element.31), channel_id=1, source_target_pairs={{0,4},{4,8},{8,12},{12,16},{16,20},{20,24},{24,28},{28,0},{1,5},{5... | collective-permute-start | bytes 1928 | tf_op jit(solution)/shard_map/ppermute | solution.py:22
  117.2 5.2 %collective-permute-start.5 = (f32[1,160,1]{2,1,0:T(8,128)S(1)}, f32[1,160,1]{2,1,0:T(8,128)S(1)}, u32[]{:S(2)}, u32[]{:S(2)}) collective-permute-start(f32[1,160,1]{2,1,0:T(8,128)S(1)} %get-tuple-element.32), channel_id=1, source_target_pairs={{4,0},{8,4},{12,8},{16,12},{20,16},{24,20},{28,24},{0,28},{5,1},{9... | collective-permute-start | bytes 1928 | tf_op jit(solution)/shard_map/ppermute | solution.py:23
  122.5 5.7 %collective-permute-start.6 = (f32[1,1,482]{2,1,0:T(1,128)S(1)}, f32[1,1,482]{2,1,0:T(1,128)S(1)}, u32[]{:S(2)}, u32[]{:S(2)}) collective-permute-start(f32[1,1,482]{2,1,0:T(1,128)S(1)} %get-tuple-element.25), channel_id=1, source_target_pairs={{0,1},{1,2},{2,3},{4,5},{5,6},{6,7},{8,9},{9,10},{10,11},{12,13},{... | collective-permute-start | bytes 5792 | tf_op jit(solution)/shard_map/ppermute | solution.py:22
  126.7 5.5 %collective-permute-start.7 = (f32[1,1,482]{2,1,0:T(1,128)S(1)}, f32[1,1,482]{2,1,0:T(1,128)S(1)}, u32[]{:S(2)}, u32[]{:S(2)}) collective-permute-start(f32[1,1,482]{2,1,0:T(1,128)S(1)} %get-tuple-element.26), channel_id=1, source_target_pairs={{1,0},{2,1},{3,2},{5,4},{6,5},{7,6},{9,8},{10,9},{11,10},{13,12},{... | collective-permute-start | bytes 5792 | tf_op jit(solution)/shard_map/ppermute | solution.py:23
  216.3 4.8 %collective-permute-start.8 = (f32[1,160,1]{2,1,0:T(8,128)S(1)}, f32[1,160,1]{2,1,0:T(8,128)S(1)}, u32[]{:S(2)}, u32[]{:S(2)}) collective-permute-start(f32[1,160,1]{2,1,0:T(8,128)S(1)} %get-tuple-element.29), channel_id=1, source_target_pairs={{0,4},{4,8},{8,12},{12,16},{16,20},{20,24},{24,28},{28,0},{1,5},{5... | collective-permute-start | bytes 1928 | tf_op jit(solution)/shard_map/ppermute | solution.py:22
  216.4 4.8 %collective-permute-start.9 = (f32[1,160,1]{2,1,0:T(8,128)S(1)}, f32[1,160,1]{2,1,0:T(8,128)S(1)}, u32[]{:S(2)}, u32[]{:S(2)}) collective-permute-start(f32[1,160,1]{2,1,0:T(8,128)S(1)} %get-tuple-element.30), channel_id=1, source_target_pairs={{4,0},{8,4},{12,8},{16,12},{20,16},{24,20},{28,24},{0,28},{5,1},{9... | collective-permute-start | bytes 1928 | tf_op jit(solution)/shard_map/ppermute | solution.py:23
  221.2 4.8 %collective-permute-start.10 = (f32[1,1,482]{2,1,0:T(1,128)S(1)}, f32[1,1,482]{2,1,0:T(1,128)S(1)}, u32[]{:S(2)}, u32[]{:S(2)}) collective-permute-start(f32[1,1,482]{2,1,0:T(1,128)S(1)} %get-tuple-element.23), channel_id=1, source_target_pairs={{0,1},{1,2},{2,3},{4,5},{5,6},{6,7},{8,9},{9,10},{10,11},{12,13},{... | collective-permute-start | bytes 5792 | tf_op jit(solution)/shard_map/ppermute | solution.py:22
  224.7 5.5 %collective-permute-start.11 = (f32[1,1,482]{2,1,0:T(1,128)S(1)}, f32[1,1,482]{2,1,0:T(1,128)S(1)}, u32[]{:S(2)}, u32[]{:S(2)}) collective-permute-start(f32[1,1,482]{2,1,0:T(1,128)S(1)} %get-tuple-element.24), channel_id=1, source_target_pairs={{1,0},{2,1},{3,2},{5,4},{6,5},{7,6},{9,8},{10,9},{11,10},{13,12},{... | collective-permute-start | bytes 5792 | tf_op jit(solution)/shard_map/ppermute | solution.py:23
  315.7 4.8 %collective-permute-start.12 = (f32[1,160,1]{2,1,0:T(8,128)S(1)}, f32[1,160,1]{2,1,0:T(8,128)S(1)}, u32[]{:S(2)}, u32[]{:S(2)}) collective-permute-start(f32[1,160,1]{2,1,0:T(8,128)S(1)} %get-tuple-element.27), channel_id=1, source_target_pairs={{0,4},{4,8},{8,12},{12,16},{16,20},{20,24},{24,28},{28,0},{1,5},{5... | collective-permute-start | bytes 1928 | tf_op jit(solution)/shard_map/ppermute | solution.py:22
  315.8 4.8 %collective-permute-start.13 = (f32[1,160,1]{2,1,0:T(8,128)S(1)}, f32[1,160,1]{2,1,0:T(8,128)S(1)}, u32[]{:S(2)}, u32[]{:S(2)}) collective-permute-start(f32[1,160,1]{2,1,0:T(8,128)S(1)} %get-tuple-element.28), channel_id=1, source_target_pairs={{4,0},{8,4},{12,8},{16,12},{20,16},{24,20},{28,24},{0,28},{5,1},{9... | collective-permute-start | bytes 1928 | tf_op jit(solution)/shard_map/ppermute | solution.py:23
  320.6 4.6 %collective-permute-start.14 = (f32[1,1,482]{2,1,0:T(1,128)S(1)}, f32[1,1,482]{2,1,0:T(1,128)S(1)}, u32[]{:S(2)}, u32[]{:S(2)}) collective-permute-start(f32[1,1,482]{2,1,0:T(1,128)S(1)} %get-tuple-element.21), channel_id=1, source_target_pairs={{0,1},{1,2},{2,3},{4,5},{5,6},{6,7},{8,9},{9,10},{10,11},{12,13},{... | collective-permute-start | bytes 5792 | tf_op jit(solution)/shard_map/ppermute | solution.py:22
  323.9 5.5 %collective-permute-start.15 = (f32[1,1,482]{2,1,0:T(1,128)S(1)}, f32[1,1,482]{2,1,0:T(1,128)S(1)}, u32[]{:S(2)}, u32[]{:S(2)}) collective-permute-start(f32[1,1,482]{2,1,0:T(1,128)S(1)} %get-tuple-element.22), channel_id=1, source_target_pairs={{1,0},{2,1},{3,2},{5,4},{6,5},{7,6},{9,8},{10,9},{11,10},{13,12},{... | collective-permute-start | bytes 5792 | tf_op jit(solution)/shard_map/ppermute | solution.py:23
Sparse Core Ops, SparseCore 0:
  9.9 63.0 all-gather.2
where the time goes:
time: 380 us; the launch traced here: 379 us
  blocking collectives  199 us (52%)
  waiting for transfers between devices  86.1 us (23%)
  starting transfers between devices  30.4 us (8%)
  local copies, waits for them, and re-layouts  28.1 us (7%)
  between operations  20.9 us (6%)
  other arithmetic  14 us (4%)
    psum x3, blocking collectives, squares(): return lax.psum(jnp.sum(residual * residual), ('lon', 'lat'))  120 us
    psum x2, blocking collectives, body(): alpha = norm_now / lax.psum(jnp.sum(direction * image), ('lon', 'lat'))  79.2 us
    all_gather x1, waiting for transfers between devices, body(): lax.all_gather(blocks, 'lon', axis=0, tiled=True)  64.3 us
    ppermute x8, starting transfers between devices, extended(): before = lax.ppermute(last, axis, up)  15.7 us
    ppermute x8, starting transfers between devices, extended(): after = lax.ppermute(initial, axis, down)  14.6 us
    ppermute x8, waiting for transfers between devices, extended(): after = lax.ppermute(initial, axis, down)  12.3 us
    scatter x1, local copies, waits for them, and re-layouts, body(): empty.at[target].set(lax.all_gather(blocks, 'lon', axis=0, tiled=True))  10.2 us
    ppermute x8, waiting for transfers between devices, extended(): before = lax.ppermute(last, axis, up)  8.86 us
  transfers between devices with their start and end apart: 17, of which 9 were waited for; matrix products, arithmetic and copies ran while one was open for 1% of the time, Pallas kernels for 0%

commit v1 on v0

--- a/solution.py
+++ b/solution.py
@@ -10,6 +10,28 @@
 thermal = 0.25
 haline = 0.75
 cabbeling = 0.05
+
+
+def laid_out(blocks, dim):
+    shape = list(blocks.shape[1:])
+    shape[dim] *= blocks.shape[0]
+    return jnp.moveaxis(blocks, 0, dim).reshape(shape)
+
+
+def ring_gather(shard, axis, dim):
+    length = lax.axis_size(axis)
+    pairs = [(i, (i + 1) % length) for i in range(length)]
+    back = [(b, a) for a, b in pairs]
+    lower, upper = ([], [])
+    for step in range(length - 1):
+        if step % 2 == 0:
+            lower.append(lax.ppermute(lower[-1] if lower else shard, axis, pairs))
+        else:
+            upper.append(lax.ppermute(upper[-1] if upper else shard, axis, back))
+    blocks = jnp.stack([*lower[::-1], shard, *upper])
+    shift = lax.axis_index(axis) - len(lower)
+    blocks = blocks[(jnp.arange(length) - shift) % length]
+    return laid_out(blocks, dim)
 
 
 def extended(value, sides, width, wrap):
@@ -51,7 +73,7 @@
     landing = jnp.where(dest_all >= 0, dest_all % slots_dev, 0)
     empty = jnp.zeros((slots_dev + 1, values_blk), jnp.float32)
     target = jnp.where(owner == myself, landing, slots_dev)
-    placed = empty.at[target].set(lax.all_gather(blocks, "lon", axis=0, tiled=True))[:slots_dev]
+    placed = empty.at[target].set(ring_gather(blocks, "lon", 0))[:slots_dev]
     rows_dev = kmt.shape[0]
     cols_dev = kmt.shape[1]
     block_rows = rows_dev // BH

time: 380 us -> 430 us (1.13)
  waiting for transfers between devices: 86.1 us -> 115 us
  local copies, waits for them, and re-layouts: 28.1 us -> 51 us
  between operations: 20.9 us -> 7.51 us
  starting transfers between devices: 30.4 us -> 39.6 us
    ppermute x0 -> x7, waiting for transfers between devices: none -> 94.8 us  [the longest x4 94.8 us: ring_gather(): lower.append(lax.ppermute(lower[-1] if lower else shard, axis, pairs))]
    all_gather x1 -> x0, waiting for transfers between devices: 64.3 us -> none  [body(): lax.all_gather(blocks, 'lon', axis=0, tiled=True)]
    unnamed x14 -> x25, local copies, waits for them, and re-layouts: 2.96 us -> 16.5 us
    gather x0 -> x1, local copies, waits for them, and re-layouts: none -> 8.74 us  [ring_gather(): blocks = blocks[(jnp.arange(length) - shift) % length]]
    ppermute x0 -> x7, starting transfers between devices: none -> 7.54 us  [the longest x3 6.99 us: ring_gather(): upper.append(lax.ppermute(upper[-1] if upper else shard, axis, back))]
  transfers between devices with their start and end apart: 17 -> 23, of which waited for: 9 -> 12; matrix products, arithmetic and copies ran while one was open for 1% -> 4% of each run, Pallas kernels for 0% -> 0%
where the time goes in v1:
time: 430 us; the launch traced here: 429 us
  blocking collectives  200 us (47%)
  waiting for transfers between devices  115 us (27%)
  local copies, waits for them, and re-layouts  51 us (12%)
  starting transfers between devices  39.6 us (9%)
  other arithmetic  15.3 us (4%)
  between operations  7.51 us (2%)
    psum x3, blocking collectives, squares(): return lax.psum(jnp.sum(residual * residual), ('lon', 'lat'))  120 us
    ppermute x4, waiting for transfers between devices, ring_gather(): lower.append(lax.ppermute(lower[-1] if lower else shard, axis, pairs))  94.8 us
    psum x2, blocking collectives, body(): alpha = norm_now / lax.psum(jnp.sum(direction * image), ('lon', 'lat'))  79.6 us
    ppermute x8, starting transfers between devices, extended(): before = lax.ppermute(last, axis, up)  18.8 us
    unnamed x25, local copies, waits for them, and re-layouts  16.5 us
    ppermute x8, starting transfers between devices, extended(): after = lax.ppermute(initial, axis, down)  13.3 us
    ppermute x8, waiting for transfers between devices, extended(): after = lax.ppermute(initial, axis, down)  12.3 us
    scatter x1, local copies, waits for them, and re-layouts, body(): placed = empty.at[target].set(ring_gather(blocks, 'lon', 0))[:slots_dev]  9.6 us
  transfers between devices with their start and end apart: 23, of which 12 were waited for; matrix products, arithmetic and copies ran while one was open for 4% of the time, Pallas kernels for 0%

profile of v1, /device:TPU:0, one launch (start us, length us, event | category | flops | bytes accessed | tf_op | source)
XLA Modules:
  0.0 428.7 jit_solution(5009465108225308207)
XLA Ops:
  1.2 17.5 %collective-permute-done = f32[32,9600]{1,0:T(8,128)S(1)} collective-permute-done((f32[32,9600]{1,0:T(8,128)}, f32[32,9600]{1,0:T(8,128)S(1)}, u32[]{:S(2)}, u32[]{:S(2)}) %collective-permute-start) | collective-permute-done | bytes 1228832 | tf_op jit(solution)/shard_map/ppermute | solution.py:28
  18.7 2.6 collective-permute-start.4
  21.3 25.7 %collective-permute-done.1 = f32[32,9600]{1,0:T(8,128)S(1)} collective-permute-done((f32[32,9600]{1,0:T(8,128)S(1)}, f32[32,9600]{1,0:T(8,128)S(1)}, u32[]{:S(2)}, u32[]{:S(2)}) %collective-permute-start.1) | collective-permute-done | bytes 1228832 | tf_op jit(solution)/shard_map/ppermute | solution.py:28
  48.0 1.6 collective-permute-start.5
  49.7 26.3 %collective-permute-done.2 = f32[32,9600]{1,0:T(8,128)} collective-permute-done((f32[32,9600]{1,0:T(8,128)S(1)}, f32[32,9600]{1,0:T(8,128)}, u32[]{:S(2)}, u32[]{:S(2)}) %collective-permute-start.2) | collective-permute-done | bytes 1228832 | tf_op jit(solution)/shard_map/ppermute | solution.py:28
  77.8 2.7 collective-permute-start.6
  80.5 25.3 %collective-permute-done.3 = f32[32,9600]{1,0:T(8,128)} collective-permute-done((f32[32,9600]{1,0:T(8,128)}, f32[32,9600]{1,0:T(8,128)}, u32[]{:S(2)}, u32[]{:S(2)}) %collective-permute-start.3) | collective-permute-done | bytes 1228832 | tf_op jit(solution)/shard_map/ppermute | solution.py:28
  105.8 2.4 bitcast_dynamic-update-slice_fusion.6
  108.2 2.5 bitcast_dynamic-update-slice_fusion.5
  110.8 1.1 bitcast_dynamic-update-slice_fusion.4
  111.9 1.1 bitcast_dynamic-update-slice_fusion.3
  113.6 1.1 constant_dynamic-update-slice_fusion
  114.8 1.1 bitcast_dynamic-update-slice_fusion.2
  115.9 2.5 bitcast_dynamic-update-slice_fusion.1
  118.4 1.2 bitcast_dynamic-update-slice_fusion
  119.6 8.7 %gather_fusion = f32[8,32,9600]{2,1,0:T(8,128)} fusion(f32[8,32,9600]{2,1,0:T(8,128)} %bitcast_dynamic-update-slice_fusion, s32[1024]{0:T(1024)S(1)} %pad_clamp_fusion), kind=kCustom, calls=%fused_computation | custom fusion | bytes 19660832 | tf_op jit(solution)/shard_map/gather | solution.py:33
  128.3 9.6 %scatter_custom_fusion = f32[33,9600]{1,0:T(8,128)S(1)} fusion(s32[256]{0:T(256)S(1)} %bitcast.68, f32[256,9600]{1,0:T(8,128)} %bitcast.65, f32[]{:T(128)} %constant.67.clone.1), kind=kCustom, calls=%fused_computation.30 | custom fusion | bytes 1267712 | tf_op jit(solution)/shard_map/scatter | solution.py:76
  138.0 5.4 %reshape.212 = f32[4,8,2,2,40,60]{5,4,3,2,1,0:T(8,128)} reshape(f32[32,9600]{1,0:T(8,128)S(1)} %slice.260) | data formatting | bytes 2457600 | tf_op jit(solution)/shard_map/reshape | solution.py:81
  143.4 3.3 copy.8
  146.7 1.5 copy-done
  148.2 1.7 reshape.214
  150.0 1.6 bitcast_multiply_fusion
  153.0 2.9 reshape.213
  157.8 1.3 collective-permute-start.10
  160.0 7.0 %collective-permute-start.9 = (f32[8,1,482]{2,1,0:T(1,128)S(1)}, f32[8,1,482]{2,1,0:T(1,128)S(1)}, u32[]{:S(2)}, u32[]{:S(2)}) collective-permute-start(f32[8,1,482]{2,1,0:T(1,128)S(1)} %get-tuple-element.15), channel_id=1, source_target_pairs={{0,1},{1,2},{2,3},{4,5},{5,6},{6,7},{8,9},{9,10},{10,11},{12,13},{... | collective-permute-start | bytes 46280 | tf_op jit(solution)/shard_map/ppermute | solution.py:44
  170.1 1.4 fusion.3
  172.8 2.6 collective-permute-start.12
  175.4 2.8 collective-permute-done.11
  178.3 4.2 collective-permute-start.13
  182.5 1.5 collective-permute-start.14
  184.0 3.9 collective-permute-done.14
  188.1 1.2 multiply_reduce_fusion.3
  189.4 40.1 %all-reduce = (f32[]{:T(128)}, f32[]{:T(128)}) all-reduce(f32[]{:T(128)} %get-tuple-element.3, f32[]{:T(128)} %get-tuple-element.2), channel_id=1, replica_groups=mesh['lon'=8,'lat'=4] {'lon','lat'}, use_global_device_ids=true, to_apply=%region_3.4 | all-reduce | flops 2 | bytes 16 | tf_op jit(solution)/shard_map/psum | solution.py:63
  231.4 39.4 %psum.44 = f32[]{:T(128)} all-reduce(f32[]{:T(128)} %get-tuple-element.10), channel_id=1, replica_groups=mesh['lon'=8,'lat'=4] {'lon','lat'}, use_global_device_ids=true, to_apply=%region_8.9 | all-reduce | flops 1 | bytes 8 | tf_op jit(solution)/shard_map/psum | solution.py:63
  272.3 2.6 collective-permute-start.16
  275.0 2.1 collective-permute-done.15
  277.2 3.6 collective-permute-start.17
  280.8 1.3 collective-permute-start.18
  282.1 4.2 collective-permute-done.18
  286.4 1.2 multiply_reduce_fusion.1
  287.6 40.1 %psum.45 = f32[]{:T(128)} all-reduce(f32[]{:T(128)} %get-tuple-element.8), channel_id=1, replica_groups=mesh['lon'=8,'lat'=4] {'lon','lat'}, use_global_device_ids=true, to_apply=%region_10.11 | all-reduce | flops 1 | bytes 8 | tf_op jit(solution)/shard_map/psum | solution.py:114
  329.8 40.8 %psum.46 = f32[]{:T(128)} all-reduce(f32[]{:T(128)} %multiply_reduce_fusion), channel_id=1, replica_groups=mesh['lon'=8,'lat'=4] {'lon','lat'}, use_global_device_ids=true, to_apply=%region_12.13 | all-reduce | flops 1 | bytes 8 | tf_op jit(solution)/shard_map/psum | solution.py:63
  372.2 2.6 collective-permute-start.20
  374.8 2.1 collective-permute-done.19
  377.0 3.3 collective-permute-start.21
  380.3 1.3 collective-permute-start.22
  381.6 4.2 collective-permute-done.22
  387.1 39.4 %psum.47 = f32[]{:T(128)} all-reduce(f32[]{:T(128)} %fusion.34), channel_id=1, replica_groups=mesh['lon'=8,'lat'=4] {'lon','lat'}, use_global_device_ids=true, to_apply=%region_14.15 | all-reduce | flops 1 | bytes 8 | tf_op jit(solution)/shard_map/psum | solution.py:114
  (72 shorter events, 17.1 us)
Async XLA Ops:
  0.6 18.0 %collective-permute-start = (f32[32,9600]{1,0:T(8,128)}, f32[32,9600]{1,0:T(8,128)S(1)}, u32[]{:S(2)}, u32[]{:S(2)}) collective-permute-start(f32[32,9600]{1,0:T(8,128)} %bitcast.66), channel_id=1, source_target_pairs={{0,4},{4,8},{8,12},{12,16},{16,20},{20,24},{24,28},{28,0},{1,5},{5... | collective-permute-start | bytes 3686408 | tf_op jit(solution)/shard_map/ppermute | solution.py:28
  18.7 28.3 %collective-permute-start.1 = (f32[32,9600]{1,0:T(8,128)S(1)}, f32[32,9600]{1,0:T(8,128)S(1)}, u32[]{:S(2)}, u32[]{:S(2)}) collective-permute-start(f32[32,9600]{1,0:T(8,128)S(1)} %collective-permute-done), channel_id=1, source_target_pairs={{0,4},{4,8},{8,12},{12,16},{16,20},{20,24},{24,28},{28,0},{1,5},{5... | collective-permute-start | bytes 3686408 | tf_op jit(solution)/shard_map/ppermute | solution.py:28
  18.7 28.3 %collective-permute-start.4 = (f32[32,9600]{1,0:T(8,128)}, f32[32,9600]{1,0:T(8,128)S(1)}, u32[]{:S(2)}, u32[]{:S(2)}) collective-permute-start(f32[32,9600]{1,0:T(8,128)} %bitcast.67), channel_id=1, source_target_pairs={{4,0},{8,4},{12,8},{16,12},{20,16},{24,20},{28,24},{0,28},{5,1},{9... | collective-permute-start | bytes 3686408 | tf_op jit(solution)/shard_map/ppermute | solution.py:30
  47.0 1.0 copy-start.7
  47.0 29.0 %collective-permute-start.2 = (f32[32,9600]{1,0:T(8,128)S(1)}, f32[32,9600]{1,0:T(8,128)}, u32[]{:S(2)}, u32[]{:S(2)}) collective-permute-start(f32[32,9600]{1,0:T(8,128)S(1)} %collective-permute-done.1), channel_id=1, source_target_pairs={{0,4},{4,8},{8,12},{12,16},{16,20},{20,24},{24,28},{28,0},{1,5},{5... | collective-permute-start | bytes 3686408 | tf_op jit(solution)/shard_map/ppermute | solution.py:28
  48.0 29.8 %collective-permute-start.5 = (f32[32,9600]{1,0:T(8,128)S(1)}, f32[32,9600]{1,0:T(8,128)}, u32[]{:S(2)}, u32[]{:S(2)}) collective-permute-start(f32[32,9600]{1,0:T(8,128)S(1)} %collective-permute-done.4), channel_id=1, source_target_pairs={{4,0},{8,4},{12,8},{16,12},{20,16},{24,20},{28,24},{0,28},{5,1},{9... | collective-permute-start | bytes 3686408 | tf_op jit(solution)/shard_map/ppermute | solution.py:30
  76.0 29.8 %collective-permute-start.3 = (f32[32,9600]{1,0:T(8,128)}, f32[32,9600]{1,0:T(8,128)}, u32[]{:S(2)}, u32[]{:S(2)}) collective-permute-start(f32[32,9600]{1,0:T(8,128)} %collective-permute-done.2), channel_id=1, source_target_pairs={{0,4},{4,8},{8,12},{12,16},{16,20},{20,24},{24,28},{28,0},{1,5},{5... | collective-permute-start | bytes 3686408 | tf_op jit(solution)/shard_map/ppermute | solution.py:28
  77.8 40.6 %collective-permute-start.6 = (f32[32,9600]{1,0:T(8,128)}, f32[32,9600]{1,0:T(8,128)S(1)}, u32[]{:S(2)}, u32[]{:S(2)}) collective-permute-start(f32[32,9600]{1,0:T(8,128)} %collective-permute-done.5), channel_id=1, source_target_pairs={{4,0},{8,4},{12,8},{16,12},{20,16},{24,20},{28,24},{0,28},{5,1},{9... | collective-permute-start | bytes 3686408 | tf_op jit(solution)/shard_map/ppermute | solution.py:30
  108.2 2.5 copy-start.8
  111.9 1.7 copy-start.6
  146.7 1.5 copy-start
  150.0 1.6 copy-start.1
  152.1 3.8 collective-permute-start.7
  152.5 4.0 collective-permute-start.8
  156.8 2.3 copy-start.2
  156.8 2.3 copy-start.3
  157.8 9.2 %collective-permute-start.10 = (f32[8,1,482]{2,1,0:T(1,128)S(1)}, f32[8,1,482]{2,1,0:T(1,128)S(1)}, u32[]{:S(2)}, u32[]{:S(2)}) collective-permute-start(f32[8,1,482]{2,1,0:T(1,128)S(1)} %get-tuple-element.16), channel_id=1, source_target_pairs={{1,0},{2,1},{3,2},{5,4},{6,5},{7,6},{9,8},{10,9},{11,10},{13,12},{... | collective-permute-start | bytes 46280 | tf_op jit(solution)/shard_map/ppermute | solution.py:45
  160.0 8.5 %collective-permute-start.9 = (f32[8,1,482]{2,1,0:T(1,128)S(1)}, f32[8,1,482]{2,1,0:T(1,128)S(1)}, u32[]{:S(2)}, u32[]{:S(2)}) collective-permute-start(f32[8,1,482]{2,1,0:T(1,128)S(1)} %get-tuple-element.15), channel_id=1, source_target_pairs={{0,1},{1,2},{2,3},{4,5},{5,6},{6,7},{8,9},{9,10},{10,11},{12,13},{... | collective-permute-start | bytes 46280 | tf_op jit(solution)/shard_map/ppermute | solution.py:44
  168.8 1.3 copy-start.5
  171.6 1.1 copy-start.4
  172.7 5.5 %collective-permute-start.11 = (f32[1,160,1]{2,1,0:T(8,128)S(1)}, f32[1,160,1]{2,1,0:T(8,128)S(1)}, u32[]{:S(2)}, u32[]{:S(2)}) collective-permute-start(f32[1,160,1]{2,1,0:T(8,128)S(1)} %get-tuple-element.31), channel_id=1, source_target_pairs={{0,4},{4,8},{8,12},{12,16},{16,20},{20,24},{24,28},{28,0},{1,5},{5... | collective-permute-start | bytes 1928 | tf_op jit(solution)/shard_map/ppermute | solution.py:44
  172.8 5.4 %collective-permute-start.12 = (f32[1,160,1]{2,1,0:T(8,128)S(1)}, f32[1,160,1]{2,1,0:T(8,128)S(1)}, u32[]{:S(2)}, u32[]{:S(2)}) collective-permute-start(f32[1,160,1]{2,1,0:T(8,128)S(1)} %get-tuple-element.32), channel_id=1, source_target_pairs={{4,0},{8,4},{12,8},{16,12},{20,16},{24,20},{28,24},{0,28},{5,1},{9... | collective-permute-start | bytes 1928 | tf_op jit(solution)/shard_map/ppermute | solution.py:45
  178.3 5.7 %collective-permute-start.13 = (f32[1,1,482]{2,1,0:T(1,128)S(1)}, f32[1,1,482]{2,1,0:T(1,128)S(1)}, u32[]{:S(2)}, u32[]{:S(2)}) collective-permute-start(f32[1,1,482]{2,1,0:T(1,128)S(1)} %get-tuple-element.25), channel_id=1, source_target_pairs={{0,1},{1,2},{2,3},{4,5},{5,6},{6,7},{8,9},{9,10},{10,11},{12,13},{... | collective-permute-start | bytes 5792 | tf_op jit(solution)/shard_map/ppermute | solution.py:44
  182.5 5.5 %collective-permute-start.14 = (f32[1,1,482]{2,1,0:T(1,128)S(1)}, f32[1,1,482]{2,1,0:T(1,128)S(1)}, u32[]{:S(2)}, u32[]{:S(2)}) collective-permute-start(f32[1,1,482]{2,1,0:T(1,128)S(1)} %get-tuple-element.26), channel_id=1, source_target_pairs={{1,0},{2,1},{3,2},{5,4},{6,5},{7,6},{9,8},{10,9},{11,10},{13,12},{... | collective-permute-start | bytes 5792 | tf_op jit(solution)/shard_map/ppermute | solution.py:45
  272.3 4.8 %collective-permute-start.15 = (f32[1,160,1]{2,1,0:T(8,128)S(1)}, f32[1,160,1]{2,1,0:T(8,128)S(1)}, u32[]{:S(2)}, u32[]{:S(2)}) collective-permute-start(f32[1,160,1]{2,1,0:T(8,128)S(1)} %get-tuple-element.29), channel_id=1, source_target_pairs={{0,4},{4,8},{8,12},{12,16},{16,20},{20,24},{24,28},{28,0},{1,5},{5... | collective-permute-start | bytes 1928 | tf_op jit(solution)/shard_map/ppermute | solution.py:44
  272.3 4.8 %collective-permute-start.16 = (f32[1,160,1]{2,1,0:T(8,128)S(1)}, f32[1,160,1]{2,1,0:T(8,128)S(1)}, u32[]{:S(2)}, u32[]{:S(2)}) collective-permute-start(f32[1,160,1]{2,1,0:T(8,128)S(1)} %get-tuple-element.30), channel_id=1, source_target_pairs={{4,0},{8,4},{12,8},{16,12},{20,16},{24,20},{28,24},{0,28},{5,1},{9... | collective-permute-start | bytes 1928 | tf_op jit(solution)/shard_map/ppermute | solution.py:45
  277.2 4.9 %collective-permute-start.17 = (f32[1,1,482]{2,1,0:T(1,128)S(1)}, f32[1,1,482]{2,1,0:T(1,128)S(1)}, u32[]{:S(2)}, u32[]{:S(2)}) collective-permute-start(f32[1,1,482]{2,1,0:T(1,128)S(1)} %get-tuple-element.23), channel_id=1, source_target_pairs={{0,1},{1,2},{2,3},{4,5},{5,6},{6,7},{8,9},{9,10},{10,11},{12,13},{... | collective-permute-start | bytes 5792 | tf_op jit(solution)/shard_map/ppermute | solution.py:44
  280.8 5.5 %collective-permute-start.18 = (f32[1,1,482]{2,1,0:T(1,128)S(1)}, f32[1,1,482]{2,1,0:T(1,128)S(1)}, u32[]{:S(2)}, u32[]{:S(2)}) collective-permute-start(f32[1,1,482]{2,1,0:T(1,128)S(1)} %get-tuple-element.24), channel_id=1, source_target_pairs={{1,0},{2,1},{3,2},{5,4},{6,5},{7,6},{9,8},{10,9},{11,10},{13,12},{... | collective-permute-start | bytes 5792 | tf_op jit(solution)/shard_map/ppermute | solution.py:45
  372.1 4.8 %collective-permute-start.19 = (f32[1,160,1]{2,1,0:T(8,128)S(1)}, f32[1,160,1]{2,1,0:T(8,128)S(1)}, u32[]{:S(2)}, u32[]{:S(2)}) collective-permute-start(f32[1,160,1]{2,1,0:T(8,128)S(1)} %get-tuple-element.27), channel_id=1, source_target_pairs={{0,4},{4,8},{8,12},{12,16},{16,20},{20,24},{24,28},{28,0},{1,5},{5... | collective-permute-start | bytes 1928 | tf_op jit(solution)/shard_map/ppermute | solution.py:44
  372.2 4.8 %collective-permute-start.20 = (f32[1,160,1]{2,1,0:T(8,128)S(1)}, f32[1,160,1]{2,1,0:T(8,128)S(1)}, u32[]{:S(2)}, u32[]{:S(2)}) collective-permute-start(f32[1,160,1]{2,1,0:T(8,128)S(1)} %get-tuple-element.28), channel_id=1, source_target_pairs={{4,0},{8,4},{12,8},{16,12},{20,16},{24,20},{28,24},{0,28},{5,1},{9... | collective-permute-start | bytes 1928 | tf_op jit(solution)/shard_map/ppermute | solution.py:45
  377.0 4.6 %collective-permute-start.21 = (f32[1,1,482]{2,1,0:T(1,128)S(1)}, f32[1,1,482]{2,1,0:T(1,128)S(1)}, u32[]{:S(2)}, u32[]{:S(2)}) collective-permute-start(f32[1,1,482]{2,1,0:T(1,128)S(1)} %get-tuple-element.21), channel_id=1, source_target_pairs={{0,1},{1,2},{2,3},{4,5},{5,6},{6,7},{8,9},{9,10},{10,11},{12,13},{... | collective-permute-start | bytes 5792 | tf_op jit(solution)/shard_map/ppermute | solution.py:44
  380.3 5.5 %collective-permute-start.22 = (f32[1,1,482]{2,1,0:T(1,128)S(1)}, f32[1,1,482]{2,1,0:T(1,128)S(1)}, u32[]{:S(2)}, u32[]{:S(2)}) collective-permute-start(f32[1,1,482]{2,1,0:T(1,128)S(1)} %get-tuple-element.22), channel_id=1, source_target_pairs={{1,0},{2,1},{3,2},{5,4},{6,5},{7,6},{9,8},{10,9},{11,10},{13,12},{... | collective-permute-start | bytes 5792 | tf_op jit(solution)/shard_map/ppermute | solution.py:45
